TPU v7x, 256 devices: a whole 4x4x8 slice. The times are simulated.
256 devices in a mesh: doc: 64 (over z, y, core), tp: 4 (over x).
Axes of the slice: x: 4, y: 4, z: 8, core: 2. Of those that a mesh axis runs over, the one named last changes fastest.
Arguments:
- storage: bfloat16 [32768, 3584], P('doc', 'tp'), may hold values from -40 to 40
- row_doc: int32 [32768], P('doc'), may hold values from -1 to 63, as said below
- row_pos: int32 [32768], P('doc'), may hold values from -1 to 511, as said below
- doc_len: int32 [64], replicated, may hold values from 64 to 512, as said below
- partner: int32 [64], replicated, may hold values from 0 to 63, as said below
- norm_gain: bfloat16 [3584], replicated, may hold values from 0.25 to 1.75
- qkv_weight: bfloat16 [3584, 4608], P('doc', 'tp'), may hold values from -0.09375 to 0.09375
- qkv_bias: bfloat16 [4608], P('tp'), may hold values from -24 to 24
Outputs:
- attention: bfloat16 [65536, 3584], P('doc', 'tp')
Inputs may be any that keep to these rules, and one draw needn't show every extreme that they name: `row_doc`: the rows 0 to doc_len[d] - 1 of each document d are stored exactly once over all devices, one to a slot; -1 marks an empty slot. One device stores at most 8 rows of any one document, and exactly 8 rows of a document of 512 tokens. `row_pos`: -1 for an empty slot. `doc_len`: some document has 512 tokens and some has 64. partner[partner[d]] = d and partner[d] != d.
All inputs are finite; a program needn't handle non-finite values.
Results may differ from a plain program's by a relative error of at most 0.008.
The roundings to bfloat16 on the way count: a program that leaves them out, or rounds other values in their place, can miss the bound.
Values may be sent and summed in bfloat16 or wider, within the bound.
A program may use at most 64 MiB of HBM per device.

v0:
```python
import jax
import jax.numpy as jnp
from jax import lax
from jax.sharding import PartitionSpec as P

HEADS = 28
KVH = 4
HD = 128
HALF = 512
ROPE_BASE = 1000000.0
EPSILON = 1e-06
BLOCK_ROWS = 512


def from_partner(value, axis, stride):
    mask = 2**stride
    pairs = [(source, source ^ mask) for source in range(lax.axis_size(axis))]
    return lax.ppermute(value, axis, pairs)


def pairing(partner):
    doc_ids = jnp.arange(partner.shape[0], dtype=jnp.int32)
    first_flag = (doc_ids < partner).astype(jnp.int32)
    before = jnp.cumsum(first_flag) - first_flag
    low_doc = jnp.minimum(doc_ids, partner)
    pick_mask = (low_doc[:, None] == doc_ids[None, :]).astype(jnp.int32)
    pair_index = jnp.sum(pick_mask * before[None, :], axis=1)
    scorer = 2 * pair_index + 1 - first_flag
    match_mask = (scorer[None, :] == doc_ids[:, None]).astype(jnp.int32)
    own_doc = jnp.sum(match_mask * doc_ids[None, :], axis=1)
    return (scorer, own_doc)


def rope_tables(length, head_dim):
    half_dim = head_dim // 2
    freq_ids = jnp.arange(half_dim, dtype=jnp.float32)
    inv_freq = jnp.exp(-(2.0 * freq_ids / head_dim) * jnp.log(jnp.float32(ROPE_BASE)))
    angles = jnp.arange(length, dtype=jnp.float32)[:, None] * inv_freq[None, :]
    cosine = jnp.concatenate([jnp.cos(angles), jnp.cos(angles)], axis=1)
    sine_table = jnp.concatenate([jnp.sin(angles), jnp.sin(angles)], axis=1)
    return (cosine, sine_table)


def rotate(heads, cosine, sine_table):
    widened = heads.astype(jnp.float32)
    half_dim = widened.shape[-1] // 2
    turned = jnp.concatenate([-widened[..., half_dim:], widened[..., :half_dim]], axis=-1)
    return (widened * cosine[:, None, :] + turned * sine_table[:, None, :]).astype(jnp.bfloat16)


def rms_norm(row_values, norm_gain):
    widened = row_values.astype(jnp.float32)
    inv_rms = lax.rsqrt(jnp.mean(widened * widened, axis=-1, keepdims=True) + EPSILON)
    return (widened * inv_rms * norm_gain.astype(jnp.float32)).astype(jnp.bfloat16)


def place_rows(values, dest_index, length):
    blank_rows = jnp.zeros((length,) + values.shape[1:], values.dtype)
    return blank_rows.at[dest_index].set(values, mode="drop")


def assemble(first_part, second_part, first_len):
    padded = jnp.concatenate([first_part, jnp.zeros_like(second_part)], axis=0)
    return lax.dynamic_update_slice(padded, second_part, (first_len, jnp.int32(0)))


def attention(projected, total_len, q_heads, kv_heads, head_dim):
    length = projected.shape[0]
    cosine, sine_table = rope_tables(length, head_dim)
    queries = rotate(
        projected[:, : q_heads * head_dim].reshape(length, q_heads, head_dim), cosine, sine_table
    )
    key_heads = rotate(
        projected[:, q_heads * head_dim : (q_heads + kv_heads) * head_dim].reshape(
            length, kv_heads, head_dim
        ),
        cosine,
        sine_table,
    )
    value_heads = projected[:, (q_heads + kv_heads) * head_dim :].reshape(
        length, kv_heads, head_dim
    )
    grouped = queries.reshape(length, kv_heads, q_heads // kv_heads, head_dim)
    block_length = min(BLOCK_ROWS, length)
    root_dim = jnp.sqrt(jnp.float32(head_dim))
    pieces = []
    for row_start in range(0, length, block_length):
        row_stop = row_start + block_length
        scores = (
            jnp.einsum(
                "qkgd,skd->kgqs",
                grouped[row_start:row_stop],
                key_heads[:row_stop],
                preferred_element_type=jnp.float32,
            )
            / root_dim
        )
        row_ids = jnp.arange(row_start, row_stop, dtype=jnp.int32)[:, None]
        col_ids = jnp.arange(row_stop, dtype=jnp.int32)[None, :]
        allowed = (col_ids <= row_ids) & (col_ids < total_len)
        scores = jnp.where(allowed, scores, -jnp.inf)
        largest = jnp.max(scores, axis=-1, keepdims=True)
        exponent = jnp.exp(scores - largest)
        probabilities = (exponent / jnp.sum(exponent, axis=-1, keepdims=True)).astype(jnp.bfloat16)
        mixture = jnp.einsum(
            "kgqs,skd->qkgd",
            probabilities,
            value_heads[:row_stop],
            preferred_element_type=jnp.float32,
        )
        live_rows = (jnp.arange(row_start, row_stop, dtype=jnp.int32) < total_len)[
            :, None, None, None
        ]
        mixture = jnp.where(live_rows, mixture, 0.0)
        pieces.append(mixture.astype(jnp.bfloat16).reshape(block_length, q_heads * head_dim))
    return jnp.concatenate(pieces, axis=0)


def shards(storage, row_doc, row_pos, doc_len, partner, norm_gain, qkv_weight, qkv_bias):
    pair_count = lax.axis_size("pair")
    doc_count = 2 * pair_count
    core = lax.axis_index("core")
    me_index = lax.axis_index("pair") * 2 + core
    half_rows = HALF
    per_dest = half_rows // doc_count
    scorer, own_doc = pairing(partner)
    doc_ids = jnp.arange(doc_count, dtype=jnp.int32)
    first_doc = jnp.sum(jnp.where(doc_ids == me_index, own_doc, 0))
    second_doc = jnp.sum(jnp.where(doc_ids == first_doc, partner, 0))
    first_len = jnp.sum(jnp.where(doc_ids == first_doc, doc_len, 0))
    second_len = jnp.sum(jnp.where(doc_ids == second_doc, doc_len, 0))
    total_len = first_len + second_len
    stored = row_doc >= 0
    dest_scorer = jnp.sum(
        jnp.where(row_doc[:, None] == doc_ids[None, :], scorer[None, :], 0), axis=1
    )
    onehot = ((dest_scorer[:, None] == doc_ids[None, :]) & stored[:, None]).astype(jnp.int32)
    dest_rank = jnp.sum(jnp.cumsum(onehot, axis=0) * onehot, axis=1) - 1
    dest_index = jnp.where(stored, dest_scorer * per_dest + dest_rank, doc_count * per_dest)
    send_rows = place_rows(storage, dest_index, doc_count * per_dest).reshape(
        doc_count, per_dest, storage.shape[1]
    )
    send_pos = (
        jnp.full((doc_count * per_dest,), half_rows, jnp.int32)
        .at[dest_index]
        .set(row_pos, mode="drop")
    )
    send_pos = send_pos.reshape(doc_count, per_dest)
    doc_axes = ("pair", "core")
    got_rows, got_pos = (
        lax.all_to_all(send_rows, doc_axes, split_axis=0, concat_axis=0, tiled=True),
        lax.all_to_all(send_pos, doc_axes, split_axis=0, concat_axis=0, tiled=True),
    )
    own_rows = place_rows(
        got_rows.reshape(doc_count * per_dest, storage.shape[1]), got_pos.reshape(-1), half_rows
    )
    q_heads = HEADS // lax.axis_size("tp")
    kv_heads = KVH // lax.axis_size("tp")
    bias_wide = qkv_bias.astype(jnp.float32)
    own_full = lax.all_gather(own_rows, "tp", axis=1, tiled=True)
    normed = rms_norm(own_full, norm_gain)
    mine = lax.all_gather(qkv_weight, "pair", axis=0, tiled=False)
    theirs = from_partner(mine, "core", 0)
    is_first = core == 0
    low = jnp.where(is_first, mine, theirs)
    high = jnp.where(is_first, theirs, mine)
    full_weight = jnp.stack([low, high], axis=1).reshape(-1, qkv_weight.shape[1])
    own_sum = jnp.dot(normed, full_weight, preferred_element_type=jnp.float32)
    own_proj = (own_sum + bias_wide).astype(jnp.bfloat16)
    other_proj = from_partner(own_proj, "core", 0)
    projected = assemble(own_proj, other_proj, first_len)
    return attention(projected, total_len, q_heads, kv_heads, HD)


def solution(mesh):
    doc_count, tp_count = (mesh.shape["doc"], mesh.shape["tp"])
    split = jax.sharding.Mesh(
        mesh.devices.reshape(doc_count // 2, 2, tp_count), ("pair", "core", "tp")
    )
    rows = ("pair", "core")
    placed = (P(rows, "tp"), P(rows), P(rows), P(), P(), P(), P(rows, "tp"), P("tp"))
    return jax.shard_map(
        shards, mesh=split, in_specs=placed, out_specs=P(rows, "tp"), check_vma=False
    )
```

profile of v0, /device:TPU:1, one launch (start us, length us, event | category | flops | bytes accessed | tf_op | source)
XLA Modules:
  0.0 248.7 jit_solution(14632437046160385297)
XLA Ops:
  14.2 2.6 %scatter_custom_fusion = s32[512]{0:T(512)S(1)} fusion(s32[512]{0:T(512)S(1)} %compare_select_fusion.1, s32[512]{0:T(512)} %param.10, s32[]{:T(128)} %constant.27.clone.1), kind=kCustom, calls=%fused_computation.99 | custom fusion | bytes 2560 | tf_op jit(solution)/shard_map/scatter | solution.py:146
  17.5 13.2 %all-to-all-start = ((s32[64,1,8]{2,1,0:T(1,128)}), s32[64,1,8]{2,1,0:T(1,128)S(1)}, u32[]{:S(2)}, u32[]{:S(2)}) async-start(s32[64,1,8]{2,1,0:T(1,128)} %bitcast.4), calls=%async_computation | async-start | bytes 65536 | tf_op jit(solution)/shard_map/all_to_all | solution.py:152
  30.7 4.3 %scatter_custom_fusion.1 = bf16[512,896]{1,0:T(8,128)(2,1)} fusion(s32[512]{0:T(512)S(1)} %compare_select_fusion.1, bf16[512,896]{1,0:T(8,128)(2,1)} %param.8, bf16[]{:T(256)} %constant.17.clone.1), kind=kCustom, calls=%fused_computation.65 | custom fusion | bytes 918016 | tf_op jit(solution)/shard_map/scatter | solution.py:59
  34.9 5.2 %all-to-all-done = s32[64,1,8]{2,1,0:T(1,128)S(1)} async-done(((s32[64,1,8]{2,1,0:T(1,128)}), s32[64,1,8]{2,1,0:T(1,128)S(1)}, u32[]{:S(2)}, u32[]{:S(2)}) %all-to-all-start) | async-done | bytes 2080 | tf_op jit(solution)/shard_map/all_to_all | solution.py:152
  40.1 5.1 %all-to-all-start.1 = ((bf16[64,8,896]{2,1,0:T(8,128)(2,1)}), bf16[64,8,896]{2,1,0:T(8,128)(2,1)S(1)}, u32[]{:S(2)}, u32[]{:S(2)}) async-start(bf16[64,8,896]{2,1,0:T(8,128)(2,1)} %bitcast.6), calls=%async_computation.1 | async-start | bytes 1835008 | tf_op jit(solution)/shard_map/all_to_all | solution.py:151
  46.7 24.7 %all-to-all-done.1 = bf16[64,8,896]{2,1,0:T(8,128)(2,1)S(1)} async-done(((bf16[64,8,896]{2,1,0:T(8,128)(2,1)}), bf16[64,8,896]{2,1,0:T(8,128)(2,1)S(1)}, u32[]{:S(2)}, u32[]{:S(2)}) %all-to-all-start.1) | async-done | bytes 917536 | tf_op jit(solution)/shard_map/all_to_all | solution.py:151
  71.4 3.6 %scatter_custom_fusion.2 = bf16[512,896]{1,0:T(8,128)(2,1)} fusion(s32[512]{0:T(512)S(1)} %bitcast.119, bf16[64,8,896]{2,1,0:T(8,128)(2,1)S(1)} %all-to-all-done.1, bf16[]{:T(256)} %constant.17.clone.1), kind=kCustom, calls=%fused_computation.49 | custom fusion | bytes 1835010 | tf_op jit(solution)/shard_map/scatter | solution.py:59
  75.0 18.9 %all-gather.6.cloned.1.call-done = bf16[1792,1152]{1,0:T(8,128)(2,1)} async-done(((bf16[56,1152]{1,0:T(8,128)(2,1)}), bf16[1792,1152]{1,0:T(8,128)(2,1)}) %all-gather.6.cloned.1.call-update) | async-done | bytes 4128784 | tf_op jit(solution)/shard_map/all_gather | solution.py:162
  94.0 4.2 %collective-permute-start = (bf16[32,56,1152]{2,1,0:T(8,128)(2,1)}, bf16[32,56,1152]{2,1,0:T(8,128)(2,1)}, u32[]{:S(2)}, u32[]{:S(2)}) collective-permute-start(bf16[32,56,1152]{2,1,0:T(8,128)(2,1)} %bitcast.114), channel_id=1, source_target_pairs={{0,4},{4,0},{1,5},{5,1},{2,6},{6,2},{3,7},{7,3},{8,12},{12,8},{9,1... | collective-permute-start | bytes 12386312 | tf_op jit(solution)/shard_map/ppermute | solution.py:18
  100.4 42.4 %all-gather.4.cloned.1.call-done = bf16[512,3584]{1,0:T(8,128)(2,1)} async-done(((bf16[512,896]{1,0:T(8,128)(2,1)}), bf16[512,3584]{1,0:T(8,128)(2,1)}) %all-gather.4.cloned.1.call-update) | async-done | bytes 3670032 | tf_op jit(solution)/shard_map/all_gather | solution.py:160
  142.8 2.8 %fusion.2 = f32[512]{0:T(512)S(1)} fusion(bf16[512,3584]{1,0:T(8,128)(2,1)} %all-gather.4.cloned.1.call-done), kind=kLoop, calls=%fused_computation.11 | loop fusion | flops 5504512 | bytes 3672064 | tf_op jit(solution)/shard_map/reduce_sum | solution.py:53
  145.6 5.1 %select_bitcast_fusion.1 = (bf16[32,1,56,1152]{3,2,1,0:T(8,128)(2,1)S(1)}, bf16[32,1,56,1152]{3,2,1,0:T(8,128)(2,1)}) fusion(bf16[32,56,1152]{2,1,0:T(8,128)(2,1)} %bitcast.115, bf16[32,56,1152]{2,1,0:T(8,128)(2,1)} %collective-permute-done, pred[]{:T(512)S(6)} %eq.110), kind=kLoop, calls=%fused_computation.22 | loop fusion | flops 4128768 | bytes 16515073 | tf_op jit(solution)/shard_map/stack | solution.py:167
  150.7 6.2 %pad_maximum_fusion = bf16[32,2,56,1152]{3,2,1,0:T(8,128)(2,1)} fusion(bf16[32,1,56,1152]{3,2,1,0:T(8,128)(2,1)} %get-tuple-element.8, bf16[32,1,56,1152]{3,2,1,0:T(8,128)(2,1)S(1)} %get-tuple-element.7), kind=kLoop, calls=%fused_computation.10 | loop fusion | flops 4128768 | bytes 16515072 | tf_op jit(solution)/shard_map/stack | solution.py:167
  156.9 10.4 %fusion.21 = bf16[512,1152]{1,0:T(8,128)(2,1)} fusion(bf16[3584,1152]{1,0:T(8,128)(2,1)} %bitcast.113, bf16[512,3584]{1,0:T(8,128)(2,1)} %all-gather.4.cloned.1.call-done, f32[3584]{0:T(1024)S(1)} %convert_element_type.65, f32[512]{0:T(512)S(1)} %add_rsqrt_fusion, f32[1152]{0:T(1024)S(1)} %convert_element_type.67), kind=kOutput, calls=%fused_computation.34 | convolution fusion | flops 4236378112 | bytes 13128192 | tf_op jit(solution)/shard_map/dot_general | solution.py:168
  173.7 2.8 %fusion.42 = (f32[1024,64]{1,0:T(8,128)}, f32[1024,64]{1,0:T(8,128)}) fusion(f32[64]{0:T(128)S(1)} %multiply_exponential_fusion), kind=kLoop, calls=%fused_computation.63 | loop fusion | flops 65536 | bytes 524544 | tf_op jit(solution)/shard_map/cos | solution.py:39
  178.0 7.4 %dynamic_update_slice.3 = bf16[1024,1152]{1,0:T(8,128)(2,1)S(1)} dynamic-update-slice(bf16[1024,1152]{1,0:T(8,128)(2,1)S(1)} %concatenate.23, bf16[512,1152]{1,0:T(8,128)(2,1)} %collective-permute-done.1, s32[]{:T(128)S(6)} %select_n.78, s32[]{:T(128)} %constant.24.clone.1) | dynamic-update-slice | bytes 2359300 | tf_op jit(solution)/shard_map/dynamic_update_slice | solution.py:64
  185.5 2.2 slice_convert_fusion
  188.9 5.0 %copy.50 = f32[1024,896]{0,1:T(8,128)} copy(f32[1024,896]{1,0:T(8,128)} %slice_convert_fusion) | data formatting | bytes 7340032 | tf_op jit(solution)/shard_map/convert_element_type | solution.py:45
  193.9 5.0 %copy.51 = f32[1024,7,128]{2,0,1:T(8,128)} copy(f32[1024,7,128]{0,2,1:T(8,128)} %bitcast.112) | data formatting | bytes 7340032 | tf_op jit(solution)/shard_map/convert_element_type | solution.py:45
  199.0 4.5 %slice_negate_fusion = (f32[1024,7,64]{2,0,1:T(8,128)S(1)}, f32[1024,7,64]{2,0,1:T(8,128)S(1)}) fusion(f32[1024,7,128]{2,0,1:T(8,128)} %copy.51), kind=kLoop, calls=%fused_computation.24 | loop fusion | flops 458752 | bytes 7340032 | tf_op jit(solution)/shard_map/neg | solution.py:47
  209.4 4.0 %fusion.26 = bf16[1,128,7,512]{3,1,2,0:T(8,128)(2,1)} fusion(f32[7,512]{1,0:T(8,128)S(1)} %fusion.7, f32[7,512]{1,0:T(8,128)S(1)} %get-tuple-element.22, f32[512,512,7]{1,0,2:T(8,128)S(1)} %get-tuple-element.23, pred[512,512]{0,1:T(8,128)(4,1)S(1)} %fusion.31, pred[512]{0:T(512)(128)(4,1)S(1)} %get-tuple-element.24, bf16[1024,1152]{1,0:T(8,128)(2,1)} %copy-done.1), kind=kOutput, calls=%fused_computation.42 | convolution fusion | flops 479854592 | bytes 8679936 | tf_op jit(solution)/shard_map/kgqs,skd->qkgd/dot_general | solution.py:105
  215.7 6.5 %fusion.1 = (f32[7,512]{1,0:T(8,128)S(1)}, f32[1024,512,7]{1,0,2:T(8,128)}) fusion(pred[512,1024]{0,1:T(8,128)(4,1)S(1)} %fusion.24, bf16[1024,7,128]{2,0,1:T(8,128)(2,1)S(1)} %fusion.12, bf16[1024,128]{1,0:T(8,128)(2,1)S(1)} %get-tuple-element.11), kind=kOutput, calls=%fused_computation.7 | convolution fusion | flops 950530560 | bytes 16398336 | tf_op jit(solution)/shard_map/qkgd,skd->kgqs/dot_general | solution.py:90
  222.2 8.2 %fusion = f32[7,512]{1,0:T(8,128)S(1)} fusion(f32[1024,512,7]{1,0,2:T(8,128)} %get-tuple-element.21, f32[7,512]{1,0:T(8,128)S(1)} %get-tuple-element.20, pred[512,1024]{0,1:T(8,128)(4,1)S(1)} %fusion.24), kind=kLoop, calls=%fused_computation.6 | loop fusion | flops 14676480 | bytes 15233024 | tf_op jit(solution)/shard_map/reduce_sum | solution.py:104
  230.4 8.5 %fusion.25 = bf16[1,128,7,512]{3,1,2,0:T(8,128)(2,1)} fusion(f32[7,512]{1,0:T(8,128)S(1)} %fusion, f32[7,512]{1,0:T(8,128)S(1)} %get-tuple-element.20, f32[1024,512,7]{1,0,2:T(8,128)} %get-tuple-element.21, pred[512,1024]{0,1:T(8,128)(4,1)S(1)} %fusion.24, pred[512]{0:T(512)(128)(4,1)S(1)} %get-tuple-element.25, bf16[1024,1152]{1,0:T(8,128)(2,1)} %copy-done.1), kind=kOutput, calls=%fused_computation.40 | convolution fusion | flops 958791680 | bytes 16413184 | tf_op jit(solution)/shard_map/kgqs,skd->qkgd/dot_general | solution.py:105
  (74 shorter events, 28.9 us)
Async XLA Ops:
  6.5 92.5 %copy-start.10 = (s32[64]{0:T(128)S(1)}, s32[64]{0:T(128)}, u32[]{:S(2)}) copy-start(s32[64]{0:T(128)} %param.12) | copy-start | bytes 772
  6.5 91.7 %copy-start.7 = (bf16[3584]{0:T(1024)(128)(2,1)S(1)}, bf16[3584]{0:T(1024)(128)(2,1)}, u32[]{:S(2)}) copy-start(bf16[3584]{0:T(1024)(128)(2,1)} %param.13) | copy-start | bytes 21508
  6.5 91.7 %copy-start.8 = (bf16[1152]{0:T(1024)(128)(2,1)S(1)}, bf16[1152]{0:T(1024)(128)(2,1)}, u32[]{:S(2)}) copy-start(bf16[1152]{0:T(1024)(128)(2,1)} %param.15) | copy-start | bytes 6916
  6.5 87.4 %all-gather.6.cloned.1.call-start = ((), (), s32[]{:S(2)}) async-start(), calls=%async_computation.3 | async-start | bytes 4257792 | tf_op jit(solution)/shard_map/all_gather | solution.py:162
  17.5 22.6 %all-to-all-start = ((s32[64,1,8]{2,1,0:T(1,128)}), s32[64,1,8]{2,1,0:T(1,128)S(1)}, u32[]{:S(2)}, u32[]{:S(2)}) async-start(s32[64,1,8]{2,1,0:T(1,128)} %bitcast.4), calls=%async_computation | async-start | bytes 65536 | tf_op jit(solution)/shard_map/all_to_all | solution.py:152
  40.1 31.3 %all-to-all-start.1 = ((bf16[64,8,896]{2,1,0:T(8,128)(2,1)}), bf16[64,8,896]{2,1,0:T(8,128)(2,1)S(1)}, u32[]{:S(2)}, u32[]{:S(2)}) async-start(bf16[64,8,896]{2,1,0:T(8,128)(2,1)} %bitcast.6), calls=%async_computation.1 | async-start | bytes 1835008 | tf_op jit(solution)/shard_map/all_to_all | solution.py:151
  45.2 97.5 %all-gather.4.cloned.1.call-start = ((), (), s32[]{:S(2)}) async-start(), calls=%async_computation.2 | async-start | bytes 4587520 | tf_op jit(solution)/shard_map/all_gather | solution.py:160
  94.0 51.6 %collective-permute-start = (bf16[32,56,1152]{2,1,0:T(8,128)(2,1)}, bf16[32,56,1152]{2,1,0:T(8,128)(2,1)}, u32[]{:S(2)}, u32[]{:S(2)}) collective-permute-start(bf16[32,56,1152]{2,1,0:T(8,128)(2,1)} %bitcast.114), channel_id=1, source_target_pairs={{0,4},{4,0},{1,5},{5,1},{2,6},{6,2},{3,7},{7,3},{8,12},{12,8},{9,1... | collective-permute-start | bytes 12386312 | tf_op jit(solution)/shard_map/ppermute | solution.py:18
  156.9 11.2 %copy-start.9 = (s32[64]{0:T(128)S(1)}, s32[64]{0:T(128)}, u32[]{:S(2)}) copy-start(s32[64]{0:T(128)} %param.11) | copy-start | bytes 772
  167.3 10.7 %collective-permute-start.1 = (bf16[512,1152]{1,0:T(8,128)(2,1)}, bf16[512,1152]{1,0:T(8,128)(2,1)}, u32[]{:S(2)}, u32[]{:S(2)}) collective-permute-start(bf16[512,1152]{1,0:T(8,128)(2,1)} %fusion.21), channel_id=1, source_target_pairs={{0,4},{4,0},{1,5},{5,1},{2,6},{6,2},{3,7},{7,3},{8,12},{12,8},{9,1... | collective-permute-start | bytes 3538952 | tf_op jit(solution)/shard_map/ppermute | solution.py:18
  185.5 18.0 %copy-start.1 = (bf16[1024,1152]{1,0:T(8,128)(2,1)}, bf16[1024,1152]{1,0:T(8,128)(2,1)S(1)}, u32[]{:S(2)}) copy-start(bf16[1024,1152]{1,0:T(8,128)(2,1)S(1)} %dynamic_update_slice.3) | copy-start | bytes 7077892
  199.0 4.5 %copy-start.3 = (f32[1024,64]{1,0:T(8,128)S(1)}, f32[1024,64]{1,0:T(8,128)}, u32[]{:S(2)}) copy-start(f32[1024,64]{1,0:T(8,128)} %get-tuple-element.16) | copy-start | bytes 786436
  199.0 4.5 %copy-start.4 = (f32[1024,64]{1,0:T(8,128)S(1)}, f32[1024,64]{1,0:T(8,128)}, u32[]{:S(2)}) copy-start(f32[1024,64]{1,0:T(8,128)} %get-tuple-element.17) | copy-start | bytes 786436
  199.0 4.5 %copy-start.5 = (f32[1024,64]{1,0:T(8,128)S(1)}, f32[1024,64]{1,0:T(8,128)}, u32[]{:S(2)}) copy-start(f32[1024,64]{1,0:T(8,128)} %get-tuple-element.14) | copy-start | bytes 786436
  199.0 4.5 %copy-start.6 = (f32[1024,64]{1,0:T(8,128)S(1)}, f32[1024,64]{1,0:T(8,128)}, u32[]{:S(2)}) copy-start(f32[1024,64]{1,0:T(8,128)} %get-tuple-element.15) | copy-start | bytes 786436
  203.5 2.0 copy-start
  230.4 10.1 %copy-start.2 = (bf16[512,896]{1,0:T(8,128)(2,1)S(1)}, bf16[512,896]{1,0:T(8,128)(2,1)}, u32[]{:S(2)}) copy-start(bf16[512,896]{1,0:T(8,128)(2,1)} %copy.58) | copy-start | bytes 2752516
Sparse Core Ops, SparseCore 0:
  10.0 83.9 all-gather.5
  95.8 46.9 all-gather.3
where the time goes:
time: 250 us; the launch traced here: 249 us
  waiting for transfers between devices  91.9 us (37%)
  other arithmetic  49.6 us (20%)
  local copies, waits for them, and re-layouts  36.4 us (15%)
  matrix products  30.8 us (12%)
  starting transfers between devices  23.3 us (9%)
  between operations  16.8 us (7%)
    all_gather x1, waiting for transfers between devices, shards(): own_full = lax.all_gather(own_rows, 'tp', axis=1, tiled=True)  42.4 us
    all_to_all x1, waiting for transfers between devices, shards(): lax.all_to_all(send_rows, doc_axes, split_axis=0, concat_axis=0, tiled=True)  24.7 us
    all_gather x1, waiting for transfers between devices, shards(): mine = lax.all_gather(qkv_weight, 'pair', axis=0, tiled=False)  18.9 us
    all_to_all x1, starting transfers between devices, shards(): lax.all_to_all(send_pos, doc_axes, split_axis=0, concat_axis=0, tiled=True)  13.2 us
    dot_general x2, matrix products, attention(): jnp.einsum('kgqs,skd->qkgd', probabilities, value_heads[:row_stop], prefe...  12.6 us
    another operation x2, other arithmetic, shards(): jnp.stack([low, high], axis=1).reshape(-1, qkv_weight.shape[1])  11.3 us
    dot_general x1, matrix products, shards(): own_sum = jnp.dot(normed, full_weight, preferred_element_type=jnp.float32)  10.4 us
    convert_element_type x2, local copies, waits for them, and re-layouts, rotate(): widened = heads.astype(jnp.float32)  10.1 us
  transfers between devices with their start and end apart: 6, of which 4 were waited for; matrix products, arithmetic and copies ran while one was open for 12% of the time, Pallas kernels for 0%

commit v1 on v0

--- a/solution.py
+++ b/solution.py
@@ -157,7 +157,9 @@
     q_heads = HEADS // lax.axis_size("tp")
     kv_heads = KVH // lax.axis_size("tp")
     bias_wide = qkv_bias.astype(jnp.float32)
-    own_full = lax.all_gather(own_rows, "tp", axis=1, tiled=True)
+    own_full = jnp.concatenate(
+        lax.all_to_all(jnp.stack([own_rows] * lax.axis_size("tp")), "tp", 0, 0), axis=1
+    )
     normed = rms_norm(own_full, norm_gain)
     mine = lax.all_gather(qkv_weight, "pair", axis=0, tiled=False)
     theirs = from_partner(mine, "core", 0)

time: 250 us -> 264 us (1.056)
  starting transfers between devices: 23.3 us -> 28.6 us
  waiting for transfers between devices: 91.9 us -> 95.6 us
  other arithmetic: 49.6 us -> 52.4 us
    all_gather x1 -> x0, waiting for transfers between devices: 42.4 us -> none  [shards(): own_full = lax.all_gather(own_rows, 'tp', axis=1, tiled=True)]
    all_to_all x0 -> x1, waiting for transfers between devices: none -> 41 us  [shards(): lax.all_to_all(jnp.stack([own_rows] * lax.axis_size('tp')), 'tp', 0, 0)]
    all_gather x1, waiting for transfers between devices: 18.9 us -> 48.7 us  [shards(): mine = lax.all_gather(qkv_weight, 'pair', axis=0, tiled=False)]
    all_to_all x1, waiting for transfers between devices: 24.7 us -> 0.01 us  [shards(): lax.all_to_all(send_rows, doc_axes, split_axis=0, concat_axis=0, tiled=True)]
    all_to_all x0 -> x1, starting transfers between devices: none -> 5.11 us  [shards(): lax.all_to_all(jnp.stack([own_rows] * lax.axis_size('tp')), 'tp', 0, 0)]
    convert_element_type x1, other arithmetic: 0.01 us -> 3.95 us  [rms_norm(): (widened * inv_rms * norm_gain.astype(jnp.float32)).astype(jnp.bfloat16)]
    scatter x2 -> x3, local copies, waits for them, and re-layouts: 7.91 us -> 7.74 us  [place_rows(): return blank_rows.at[dest_index].set(values, mode='drop')]
  transfers between devices with their start and end apart: 6 -> 6, of which waited for: 4 -> 3; matrix products, arithmetic and copies ran while one was open for 12% -> 14% of each run, Pallas kernels for 0% -> 0%
where the time goes in v1:
time: 264 us; the launch traced here: 262 us
  waiting for transfers between devices  95.6 us (36%)
  other arithmetic  52.4 us (20%)
  local copies, waits for them, and re-layouts  38.3 us (15%)
  matrix products  30.8 us (12%)
  starting transfers between devices  28.6 us (11%)
  between operations  16.8 us (6%)
    all_gather x1, waiting for transfers between devices, shards(): mine = lax.all_gather(qkv_weight, 'pair', axis=0, tiled=False)  48.7 us
    all_to_all x1, waiting for transfers between devices, shards(): lax.all_to_all(jnp.stack([own_rows] * lax.axis_size('tp')), 'tp', 0, 0)  41 us
    all_to_all x1, starting transfers between devices, shards(): lax.all_to_all(send_pos, doc_axes, split_axis=0, concat_axis=0, tiled=True)  13.2 us
    dot_general x2, matrix products, attention(): jnp.einsum('kgqs,skd->qkgd', probabilities, value_heads[:row_stop], prefe...  12.6 us
    dot_general x1, matrix products, shards(): own_sum = jnp.dot(normed, full_weight, preferred_element_type=jnp.float32)  10.4 us
    another operation x2, other arithmetic, shards(): jnp.stack([low, high], axis=1).reshape(-1, qkv_weight.shape[1])  10.1 us
    convert_element_type x2, local copies, waits for them, and re-layouts, rotate(): widened = heads.astype(jnp.float32)  10.1 us
    reduce_sum x2, other arithmetic, attention(): jnp.sum(exponent, axis=-1, keepdims=True)  9.7 us
  transfers between devices with their start and end apart: 6, of which 3 were waited for; matrix products, arithmetic and copies ran while one was open for 14% of the time, Pallas kernels for 0%

profile of v1, /device:TPU:1, one launch (start us, length us, event | category | flops | bytes accessed | tf_op | source)
XLA Modules:
  0.0 262.5 jit_solution(10474192305787739962)
XLA Ops:
  14.2 2.6 scatter_custom_fusion
  17.5 13.2 %all-to-all-start = ((s32[64,1,8]{2,1,0:T(1,128)}), s32[64,1,8]{2,1,0:T(1,128)S(1)}, u32[]{:S(2)}, u32[]{:S(2)}) async-start(s32[64,1,8]{2,1,0:T(1,128)} %bitcast.4), calls=%async_computation | async-start | bytes 65536 | tf_op jit(solution)/shard_map/all_to_all | solution.py:152
  30.7 4.3 %scatter_custom_fusion.1 = bf16[512,896]{1,0:T(8,128)(2,1)} fusion(s32[512]{0:T(512)S(1)} %compare_select_fusion.1, bf16[512,896]{1,0:T(8,128)(2,1)} %param.8, bf16[]{:T(256)} %constant.17.clone.1), kind=kCustom, calls=%fused_computation.62 | custom fusion | bytes 918016 | tf_op jit(solution)/shard_map/scatter | solution.py:59
  34.9 5.2 %all-to-all-done = s32[64,1,8]{2,1,0:T(1,128)S(1)} async-done(((s32[64,1,8]{2,1,0:T(1,128)}), s32[64,1,8]{2,1,0:T(1,128)S(1)}, u32[]{:S(2)}, u32[]{:S(2)}) %all-to-all-start) | async-done | bytes 2080 | tf_op jit(solution)/shard_map/all_to_all | solution.py:152
  40.1 5.1 %all-to-all-start.1 = ((bf16[64,8,896]{2,1,0:T(8,128)(2,1)}), bf16[64,8,896]{2,1,0:T(8,128)(2,1)S(1)}, u32[]{:S(2)}, u32[]{:S(2)}) async-start(bf16[64,8,896]{2,1,0:T(8,128)(2,1)} %bitcast.6), calls=%async_computation.1 | async-start | bytes 1835008 | tf_op jit(solution)/shard_map/all_to_all | solution.py:151
  45.2 48.7 %all-gather.3.cloned.1.call-done = bf16[1792,1152]{1,0:T(8,128)(2,1)} async-done(((bf16[56,1152]{1,0:T(8,128)(2,1)}), bf16[1792,1152]{1,0:T(8,128)(2,1)}) %all-gather.3.cloned.1.call-update) | async-done | bytes 4128784 | tf_op jit(solution)/shard_map/all_gather | solution.py:164
  94.0 4.4 %collective-permute-start = (bf16[32,56,1152]{2,1,0:T(8,128)(2,1)}, bf16[32,56,1152]{2,1,0:T(8,128)(2,1)}, u32[]{:S(2)}, u32[]{:S(2)}) collective-permute-start(bf16[32,56,1152]{2,1,0:T(8,128)(2,1)} %bitcast.118), channel_id=1, source_target_pairs={{0,4},{4,0},{1,5},{5,1},{2,6},{6,2},{3,7},{7,3},{8,12},{12,8},{9,1... | collective-permute-start | bytes 12386312 | tf_op jit(solution)/shard_map/ppermute | solution.py:18
  99.6 2.9 %scatter_custom_fusion.2 = bf16[512,896]{1,0:T(8,128)(2,1)S(1)} fusion(s32[512]{0:T(512)S(1)} %bitcast.124, bf16[64,8,896]{2,1,0:T(8,128)(2,1)S(1)} %all-to-all-done.1, bf16[]{:T(256)} %constant.17.clone.1), kind=kCustom, calls=%fused_computation.46 | custom fusion | bytes 1835010 | tf_op jit(solution)/shard_map/scatter | solution.py:59
  105.3 5.1 %all-to-all-start.2 = ((bf16[4,512,896]{1,2,0:T(8,128)(2,1)}), bf16[4,512,896]{1,2,0:T(8,128)(2,1)}, u32[]{:S(2)}, u32[]{:S(2)}) async-start(bf16[4,512,896]{1,2,0:T(8,128)(2,1)} %stack.16), calls=%async_computation.2 | async-start | bytes 7340032 | tf_op jit(solution)/shard_map/all_to_all | solution.py:161
  112.6 41.0 %all-to-all-done.2 = bf16[4,512,896]{1,2,0:T(8,128)(2,1)} async-done(((bf16[4,512,896]{1,2,0:T(8,128)(2,1)}), bf16[4,512,896]{1,2,0:T(8,128)(2,1)}, u32[]{:S(2)}, u32[]{:S(2)}) %all-to-all-start.2) | async-done | bytes 3670048 | tf_op jit(solution)/shard_map/all_to_all | solution.py:161
  153.6 2.9 %fusion.2 = f32[512]{0:T(512)S(1)} fusion(bf16[4,512,896]{1,2,0:T(8,128)(2,1)} %all-to-all-done.2), kind=kLoop, calls=%fused_computation.11 | loop fusion | flops 5504512 | bytes 3672064 | tf_op jit(solution)/shard_map/reduce_sum | solution.py:53
  156.5 4.0 %fusion.4 = bf16[4,512,896]{1,2,0:T(8,128)(2,1)} fusion(bf16[4,512,896]{1,2,0:T(8,128)(2,1)} %all-to-all-done.2, f32[4,896]{1,0:T(4,128)S(1)} %reshape.238, f32[512]{0:T(512)S(1)} %add_rsqrt_fusion), kind=kLoop, calls=%fused_computation.13 | loop fusion | flops 7340032 | bytes 7356416 | tf_op jit(solution)/shard_map/convert_element_type | solution.py:54
  160.5 3.9 %select_bitcast_fusion.1 = (bf16[32,1,56,1152]{3,2,1,0:T(8,128)(2,1)S(1)}, bf16[32,1,56,1152]{3,2,1,0:T(8,128)(2,1)}) fusion(bf16[32,56,1152]{2,1,0:T(8,128)(2,1)S(1)} %bitcast.119, bf16[32,56,1152]{2,1,0:T(8,128)(2,1)} %collective-permute-done, pred[]{:T(512)S(6)} %eq.110), kind=kLoop, calls=%fused_computation.22 | loop fusion | flops 4128768 | bytes 16515073 | tf_op jit(solution)/shard_map/stack | solution.py:169
  164.4 6.2 %pad_maximum_fusion = bf16[32,2,56,1152]{3,2,1,0:T(8,128)(2,1)} fusion(bf16[32,1,56,1152]{3,2,1,0:T(8,128)(2,1)} %get-tuple-element.8, bf16[32,1,56,1152]{3,2,1,0:T(8,128)(2,1)S(1)} %get-tuple-element.7), kind=kLoop, calls=%fused_computation.10 | loop fusion | flops 4128768 | bytes 16515072 | tf_op jit(solution)/shard_map/stack | solution.py:169
  170.6 10.4 %fusion.14 = bf16[512,1152]{1,0:T(8,128)(2,1)} fusion(bf16[512,3584]{0,1:T(8,128)(2,1)} %bitcast.120, bf16[3584,1152]{1,0:T(8,128)(2,1)} %bitcast.117, f32[1152]{0:T(1024)S(1)} %convert_element_type.75), kind=kOutput, calls=%fused_computation.31 | convolution fusion | flops 4229038080 | bytes 13111808 | tf_op jit(solution)/shard_map/dot_general | solution.py:170
  187.5 2.8 %fusion.33 = (f32[1024,64]{1,0:T(8,128)}, f32[1024,64]{1,0:T(8,128)}) fusion(f32[64]{0:T(128)S(1)} %multiply_exponential_fusion), kind=kLoop, calls=%fused_computation.60 | loop fusion | flops 65536 | bytes 524544 | tf_op jit(solution)/shard_map/cos | solution.py:39
  191.8 7.4 %dynamic_update_slice.3 = bf16[1024,1152]{1,0:T(8,128)(2,1)S(1)} dynamic-update-slice(bf16[1024,1152]{1,0:T(8,128)(2,1)S(1)} %concatenate.23, bf16[512,1152]{1,0:T(8,128)(2,1)} %collective-permute-done.1, s32[]{:T(128)S(6)} %select_n.78, s32[]{:T(128)} %constant.24.clone.1) | dynamic-update-slice | bytes 2359300 | tf_op jit(solution)/shard_map/dynamic_update_slice | solution.py:64
  202.7 5.0 %copy.53 = f32[1024,896]{0,1:T(8,128)} copy(f32[1024,896]{1,0:T(8,128)} %slice_convert_fusion) | data formatting | bytes 7340032 | tf_op jit(solution)/shard_map/convert_element_type | solution.py:45
  207.7 5.0 %copy.54 = f32[1024,7,128]{2,0,1:T(8,128)} copy(f32[1024,7,128]{0,2,1:T(8,128)} %bitcast.116) | data formatting | bytes 7340032 | tf_op jit(solution)/shard_map/convert_element_type | solution.py:45
  212.8 4.5 %slice_negate_fusion = (f32[1024,7,64]{2,0,1:T(8,128)S(1)}, f32[1024,7,64]{2,0,1:T(8,128)S(1)}) fusion(f32[1024,7,128]{2,0,1:T(8,128)} %copy.54), kind=kLoop, calls=%fused_computation.23 | loop fusion | flops 458752 | bytes 7340032 | tf_op jit(solution)/shard_map/neg | solution.py:47
  223.2 4.0 %fusion.17 = bf16[1,128,7,512]{3,1,2,0:T(8,128)(2,1)} fusion(f32[7,512]{1,0:T(8,128)S(1)} %fusion.7, f32[7,512]{1,0:T(8,128)S(1)} %get-tuple-element.22, f32[512,512,7]{1,0,2:T(8,128)S(1)} %get-tuple-element.23, pred[512,512]{0,1:T(8,128)(4,1)S(1)} %fusion.22, pred[512]{0:T(512)(128)(4,1)S(1)} %get-tuple-element.24, bf16[1024,1152]{1,0:T(8,128)(2,1)} %copy-done.1), kind=kOutput, calls=%fused_computation.39 | convolution fusion | flops 479854592 | bytes 8679936 | tf_op jit(solution)/shard_map/kgqs,skd->qkgd/dot_general | solution.py:105
  229.5 6.5 %fusion.1 = (f32[7,512]{1,0:T(8,128)S(1)}, f32[1024,512,7]{1,0,2:T(8,128)}) fusion(pred[512,1024]{0,1:T(8,128)(4,1)S(1)} %fusion.15, bf16[1024,7,128]{2,0,1:T(8,128)(2,1)S(1)} %fusion.10, bf16[1024,128]{1,0:T(8,128)(2,1)S(1)} %get-tuple-element.11), kind=kOutput, calls=%fused_computation.7 | convolution fusion | flops 950530560 | bytes 16398336 | tf_op jit(solution)/shard_map/qkgd,skd->kgqs/dot_general | solution.py:90
  236.0 8.2 %fusion = f32[7,512]{1,0:T(8,128)S(1)} fusion(f32[1024,512,7]{1,0,2:T(8,128)} %get-tuple-element.21, f32[7,512]{1,0:T(8,128)S(1)} %get-tuple-element.20, pred[512,1024]{0,1:T(8,128)(4,1)S(1)} %fusion.15), kind=kLoop, calls=%fused_computation.6 | loop fusion | flops 14676480 | bytes 15233024 | tf_op jit(solution)/shard_map/reduce_sum | solution.py:104
  244.2 8.5 %fusion.16 = bf16[1,128,7,512]{3,1,2,0:T(8,128)(2,1)} fusion(f32[7,512]{1,0:T(8,128)S(1)} %fusion, f32[7,512]{1,0:T(8,128)S(1)} %get-tuple-element.20, f32[1024,512,7]{1,0,2:T(8,128)} %get-tuple-element.21, pred[512,1024]{0,1:T(8,128)(4,1)S(1)} %fusion.15, pred[512]{0:T(512)(128)(4,1)S(1)} %get-tuple-element.25, bf16[1024,1152]{1,0:T(8,128)(2,1)} %copy-done.1), kind=kOutput, calls=%fused_computation.37 | convolution fusion | flops 958791680 | bytes 16413184 | tf_op jit(solution)/shard_map/kgqs,skd->qkgd/dot_general | solution.py:105
  (78 shorter events, 33.7 us)
Async XLA Ops:
  6.5 87.4 %all-gather.3.cloned.1.call-start = ((), (), s32[]{:S(2)}) async-start(), calls=%async_computation.3 | async-start | bytes 4257792 | tf_op jit(solution)/shard_map/all_gather | solution.py:164
  17.5 22.6 %all-to-all-start = ((s32[64,1,8]{2,1,0:T(1,128)}), s32[64,1,8]{2,1,0:T(1,128)S(1)}, u32[]{:S(2)}, u32[]{:S(2)}) async-start(s32[64,1,8]{2,1,0:T(1,128)} %bitcast.4), calls=%async_computation | async-start | bytes 65536 | tf_op jit(solution)/shard_map/all_to_all | solution.py:152
  40.1 59.5 %all-to-all-start.1 = ((bf16[64,8,896]{2,1,0:T(8,128)(2,1)}), bf16[64,8,896]{2,1,0:T(8,128)(2,1)S(1)}, u32[]{:S(2)}, u32[]{:S(2)}) async-start(bf16[64,8,896]{2,1,0:T(8,128)(2,1)} %bitcast.6), calls=%async_computation.1 | async-start | bytes 1835008 | tf_op jit(solution)/shard_map/all_to_all | solution.py:151
  94.0 66.5 %collective-permute-start = (bf16[32,56,1152]{2,1,0:T(8,128)(2,1)}, bf16[32,56,1152]{2,1,0:T(8,128)(2,1)}, u32[]{:S(2)}, u32[]{:S(2)}) collective-permute-start(bf16[32,56,1152]{2,1,0:T(8,128)(2,1)} %bitcast.118), channel_id=1, source_target_pairs={{0,4},{4,0},{1,5},{5,1},{2,6},{6,2},{3,7},{7,3},{8,12},{12,8},{9,1... | collective-permute-start | bytes 12386312 | tf_op jit(solution)/shard_map/ppermute | solution.py:18
  105.3 5.1 %copy-start.8 = (bf16[3584]{0:T(1024)(128)(2,1)S(1)}, bf16[3584]{0:T(1024)(128)(2,1)}, u32[]{:S(2)}) copy-start(bf16[3584]{0:T(1024)(128)(2,1)} %param.13) | copy-start | bytes 21508
  105.3 5.2 %copy-start.9 = (bf16[1152]{0:T(1024)(128)(2,1)S(1)}, bf16[1152]{0:T(1024)(128)(2,1)}, u32[]{:S(2)}) copy-start(bf16[1152]{0:T(1024)(128)(2,1)} %param.15) | copy-start | bytes 6916
  105.3 6.0 %copy-start.11 = (s32[64]{0:T(128)S(1)}, s32[64]{0:T(128)}, u32[]{:S(2)}) copy-start(s32[64]{0:T(128)} %param.12) | copy-start | bytes 772
  105.3 48.4 %all-to-all-start.2 = ((bf16[4,512,896]{1,2,0:T(8,128)(2,1)}), bf16[4,512,896]{1,2,0:T(8,128)(2,1)}, u32[]{:S(2)}, u32[]{:S(2)}) async-start(bf16[4,512,896]{1,2,0:T(8,128)(2,1)} %stack.16), calls=%async_computation.2 | async-start | bytes 7340032 | tf_op jit(solution)/shard_map/all_to_all | solution.py:161
  156.5 4.0 %copy-start.2 = (bf16[1792,1152]{1,0:T(8,128)(2,1)S(1)}, bf16[1792,1152]{1,0:T(8,128)(2,1)}, u32[]{:S(2)}) copy-start(bf16[1792,1152]{1,0:T(8,128)(2,1)} %all-gather.3.cloned.1.call-done) | copy-start | bytes 12386308
  170.6 11.2 %copy-start.10 = (s32[64]{0:T(128)S(1)}, s32[64]{0:T(128)}, u32[]{:S(2)}) copy-start(s32[64]{0:T(128)} %param.11) | copy-start | bytes 772
  181.0 10.8 %collective-permute-start.1 = (bf16[512,1152]{1,0:T(8,128)(2,1)}, bf16[512,1152]{1,0:T(8,128)(2,1)}, u32[]{:S(2)}, u32[]{:S(2)}) collective-permute-start(bf16[512,1152]{1,0:T(8,128)(2,1)} %fusion.14), channel_id=1, source_target_pairs={{0,4},{4,0},{1,5},{5,1},{2,6},{6,2},{3,7},{7,3},{8,12},{12,8},{9,1... | collective-permute-start | bytes 3538952 | tf_op jit(solution)/shard_map/ppermute | solution.py:18
  199.2 18.0 %copy-start.1 = (bf16[1024,1152]{1,0:T(8,128)(2,1)}, bf16[1024,1152]{1,0:T(8,128)(2,1)S(1)}, u32[]{:S(2)}) copy-start(bf16[1024,1152]{1,0:T(8,128)(2,1)S(1)} %dynamic_update_slice.3) | copy-start | bytes 7077892
  212.7 4.5 %copy-start.4 = (f32[1024,64]{1,0:T(8,128)S(1)}, f32[1024,64]{1,0:T(8,128)}, u32[]{:S(2)}) copy-start(f32[1024,64]{1,0:T(8,128)} %get-tuple-element.16) | copy-start | bytes 786436
  212.7 4.5 %copy-start.5 = (f32[1024,64]{1,0:T(8,128)S(1)}, f32[1024,64]{1,0:T(8,128)}, u32[]{:S(2)}) copy-start(f32[1024,64]{1,0:T(8,128)} %get-tuple-element.17) | copy-start | bytes 786436
  212.7 4.5 %copy-start.6 = (f32[1024,64]{1,0:T(8,128)S(1)}, f32[1024,64]{1,0:T(8,128)}, u32[]{:S(2)}) copy-start(f32[1024,64]{1,0:T(8,128)} %get-tuple-element.14) | copy-start | bytes 786436
  212.7 4.5 %copy-start.7 = (f32[1024,64]{1,0:T(8,128)S(1)}, f32[1024,64]{1,0:T(8,128)}, u32[]{:S(2)}) copy-start(f32[1024,64]{1,0:T(8,128)} %get-tuple-element.15) | copy-start | bytes 786436
  217.2 2.0 copy-start
  244.2 10.1 %copy-start.3 = (bf16[512,896]{1,0:T(8,128)(2,1)S(1)}, bf16[512,896]{1,0:T(8,128)(2,1)}, u32[]{:S(2)}) copy-start(bf16[512,896]{1,0:T(8,128)(2,1)} %copy.61) | copy-start | bytes 2752516
Sparse Core Ops, SparseCore 0:
  10.0 83.9 all-gather.2
